TPU v7x, 256 devices: a whole 4x4x8 slice. The times are simulated.
256 devices in a mesh: section: 8 (over y, core), rows: 32 (over x, z).
Axes of the slice: x: 4, y: 4, z: 8, core: 2. Of those that a mesh axis runs over, the one named last changes fastest.
Arguments:
- grad_in: bfloat16 [8, 8192, 256], P('section', 'rows'), may hold values from -6 to 6
- grad_last: bfloat16 [8192, 256], P('rows'), may hold values from -6 to 6
- support: bfloat16 [8, 2, 2, 8192, 256], P('section', None, None, 'rows'), may hold values from -6 to 6
- preact: bfloat16 [8, 2, 2, 8192, 256], P('section', None, None, 'rows'), may hold values from -6 to 6
- weights: bfloat16 [8, 2, 256, 256], P('section'), may hold values from -0.375 to 0.375
- tile_vals: bfloat16 [8, 2, 3072, 128, 128], P('section', None, 'rows'), may hold values from -0.078125 to 0.078125
- tile_row: int32 [8, 2, 3072], P('section', None, 'rows'), may hold values from 0 to 1
- tile_col: int32 [8, 2, 3072], P('section', None, 'rows'), may hold values from 0 to 63, as said below
- tile_count: int32 [8, 2, 32], P('section', None, 'rows'), may hold values from 48 to 96, as said below
Outputs:
- handoff: bfloat16 [2, 8, 8192, 256], P(None, 'section', 'rows')
- init_grad: float32 [8, 2, 8192, 256], P('section', None, 'rows')
- weight_grad: float32 [8, 2, 256, 256], P('section')
Inputs may be any that keep to these rules, and one draw needn't show every extreme that they name: tile_count[s, t, d] is the number of live entries in device d's list; in every section and micro-batch some device has all 96 live. `tile_col`: for every section, micro-batch and pair of devices d and o with o != d, all entries of device d's list (live or padding) whose column tile lies in device o's rows name one and the same of o's 2 row tiles.
All inputs are finite; a program needn't handle non-finite values.
Results may differ from a plain program's by a relative error of at most 0.0066.
Values may be sent and summed in bfloat16 or wider, within the bound.
A program may use at most 128 MiB of HBM per device.

v0:
```python
import jax
import jax.numpy as jnp
from jax import lax
from jax.sharding import PartitionSpec as P

ALPHA = 0.1
BETA_SCALE = 0.5


def passed_along(block, axis, distance):
    devices = range(lax.axis_size(axis))
    route = [(i - distance, i) for i in devices if i - distance in devices]
    return lax.ppermute(block, axis, route)


def tile_product(gathered, values, row_local, index, count, row_tiles):
    tile = values.shape[-1]
    width = gathered.shape[-1]
    blocks = gathered.reshape(-1, tile, width)[index]
    products = jnp.einsum("kab,kbf->kaf", values, blocks, preferred_element_type=jnp.float32)
    live = jnp.arange(index.shape[0]) < count
    select = ((row_local[None, :] == jnp.arange(row_tiles)[:, None]) & live[None, :]).astype(
        jnp.float32
    )
    summed = jnp.einsum("ik,kaf->iaf", select, products, precision=lax.Precision.HIGHEST)
    return summed.reshape(row_tiles * tile, width)


def shards(grad_in, grad_last, support, preact, weights, tile_vals, tile_row, tile_col, tile_count):
    section = lax.axis_index("section")
    sections = lax.axis_size("section")
    ticks = support.shape[1]
    layers = support.shape[2]
    rows_dev, width = grad_last.shape
    tile = tile_vals.shape[-1]
    row_tiles = rows_dev // tile
    weight_acc = [jnp.zeros((width, width), jnp.float32) for layer in range(layers)]
    handed = []
    initial = []
    for tick in range(ticks):
        if tick == 0:
            grad = grad_in[0]
        else:
            passed = passed_along(handed[-1], "section", -1)
            grad = jnp.where(section == sections - 1, grad_last, passed)
        columns = tile_col[0, tick]
        count = tile_count[0, tick, 0]
        toward = jnp.zeros((rows_dev, width), jnp.float32)
        for layer in reversed(range(layers)):
            beta = jnp.log(BETA_SCALE / (layers * section + layer + 1).astype(jnp.float32) + 1.0)
            weight = weights[0, layer]
            masked = jnp.where(preact[0, tick, layer] > 0, grad, jnp.zeros_like(grad))
            term = beta * jnp.dot(
                support[0, tick, layer].T, masked, preferred_element_type=jnp.float32
            )
            weight_acc[layer] = weight_acc[layer] + lax.psum(term, "rows")
            image = (
                (1.0 - beta) * masked.astype(jnp.float32)
                + beta * jnp.dot(masked, weight.T, preferred_element_type=jnp.float32)
            ).astype(jnp.bfloat16)
            toward = toward + ALPHA * image.astype(jnp.float32)
            gathered = lax.all_gather(image, "rows", axis=0, tiled=True)
            spread = tile_product(
                gathered, tile_vals[0, tick], tile_row[0, tick], columns, count, row_tiles
            )
            grad = ((1.0 - ALPHA) * spread).astype(jnp.bfloat16)
        handed.append(grad)
        initial.append(toward)
    return (jnp.stack(handed)[:, None], jnp.stack(initial)[None], jnp.stack(weight_acc)[None])


def solution(mesh):
    return jax.shard_map(
        shards,
        mesh=mesh,
        in_specs=(
            P("section", "rows", None),
            P("rows", None),
            P("section", None, None, "rows", None),
            P("section", None, None, "rows", None),
            P("section", None, None, None),
            P("section", None, "rows", None, None),
            P("section", None, "rows"),
            P("section", None, "rows"),
            P("section", None, "rows"),
        ),
        out_specs=(
            P(None, "section", "rows", None),
            P("section", None, "rows", None),
            P("section", None, None, None),
        ),
        check_vma=False,
    )
```

profile of v0, /device:TPU:8, one launch (start us, length us, event | category | flops | bytes accessed | tf_op | source)
XLA Modules:
  0.0 648.4 jit_solution(17739819495514293798)
XLA Ops:
  7.2 0.0 all-gather.5.cloned.1.call-start
  7.3 2.1 fusion.15
  9.4 0.0 all-gather.5.cloned.1.call-update
  9.4 0.0 all-gather.7.cloned.1.call-start
  9.5 1.3 fusion.83
  10.8 0.6 iota_compare_fusion.1
  11.5 0.8 fusion.72
  12.3 0.8 slice_bitcast_fusion
  13.0 82.8 %all-gather.5.cloned.1.call-done = bf16[8192,256]{1,0:T(8,128)(2,1)} async-done(((bf16[256,256]{1,0:T(8,128)(2,1)}), bf16[8192,256]{1,0:T(8,128)(2,1)}) %all-gather.5.cloned.1.call-update) | async-done | bytes 4194320 | tf_op jit(solution)/shard_map/all_gather | solution.py:62
  95.8 8.1 %gather_fusion = bf16[96,128,256]{2,1,0:T(8,128)(2,1)} fusion(bf16[64,128,256]{2,1,0:T(8,128)(2,1)} %bitcast.141, s32[1024]{0:T(1024)S(1)} %pad_clamp_fusion.1), kind=kCustom, calls=%fused_computation | custom fusion | bytes 12583296 | tf_op jit(solution)/shard_map/gather | solution.py:19
  103.9 10.1 %convolution_bitcast_fusion.3 = f32[96,128,256]{1,2,0:T(8,128)} fusion(bf16[96,128,256]{2,1,0:T(8,128)(2,1)} %gather_fusion, bf16[1,2,96,128,128]{4,3,2,1,0:T(8,128)(2,1)} %param.14), kind=kOutput, calls=%fused_computation.7 | convolution fusion | flops 805306368 | bytes 22020096 | tf_op jit(solution)/shard_map/kab,kbf->kaf/dot_general | solution.py:20
  114.0 12.8 %copy.38 = f32[96,128,256]{2,0,1:T(8,128)} copy(f32[96,128,256]{1,2,0:T(8,128)} %convolution_bitcast_fusion.3) | data formatting | bytes 25165824 | tf_op jit(solution)/shard_map/kab,kbf->kaf/dot_general | solution.py:20
  126.7 7.1 %fusion.65 = f32[2,128,256]{2,0,1:T(2,128)S(1)} fusion(f32[96,128,256]{2,0,1:T(8,128)} %copy.38, pred[96]{0:T(512)(128)(4,1)S(1)} %iota_compare_fusion.1, s32[96]{0:T(128)S(1)} %get-tuple-element.18), kind=kOutput, calls=%fused_computation.97 | convolution fusion | flops 75497856 | bytes 12845536 | tf_op jit(solution)/shard_map/ik,kaf->iaf/dot_general | solution.py:25
  133.9 0.9 fusion.16
  134.8 0.2 all-gather.9.cloned.1.call-start
  135.0 78.9 %all-gather.7.cloned.1.call-done = bf16[8192,256]{1,0:T(8,128)(2,1)} async-done(((bf16[256,256]{1,0:T(8,128)(2,1)}), bf16[8192,256]{1,0:T(8,128)(2,1)}) %all-gather.7.cloned.1.call-update) | async-done | bytes 4194320 | tf_op jit(solution)/shard_map/all_gather | solution.py:62
  213.9 8.1 %gather_fusion.1 = bf16[96,128,256]{2,1,0:T(8,128)(2,1)} fusion(bf16[64,128,256]{2,1,0:T(8,128)(2,1)} %bitcast.144, s32[1024]{0:T(1024)S(1)} %pad_clamp_fusion.1), kind=kCustom, calls=%fused_computation.1 | custom fusion | bytes 12583296 | tf_op jit(solution)/shard_map/gather | solution.py:19
  222.0 10.1 %convolution_bitcast_fusion.2 = f32[96,128,256]{1,2,0:T(8,128)} fusion(bf16[96,128,256]{2,1,0:T(8,128)(2,1)} %gather_fusion.1, bf16[1,2,96,128,128]{4,3,2,1,0:T(8,128)(2,1)} %param.14), kind=kOutput, calls=%fused_computation.6 | convolution fusion | flops 805306368 | bytes 22020096 | tf_op jit(solution)/shard_map/kab,kbf->kaf/dot_general | solution.py:20
  232.1 12.8 %copy.41 = f32[96,128,256]{2,0,1:T(8,128)} copy(f32[96,128,256]{1,2,0:T(8,128)} %convolution_bitcast_fusion.2) | data formatting | bytes 25165824 | tf_op jit(solution)/shard_map/kab,kbf->kaf/dot_general | solution.py:20
  244.9 7.1 %fusion.63 = f32[2,128,256]{2,0,1:T(2,128)S(1)} fusion(f32[96,128,256]{2,0,1:T(8,128)} %copy.41, pred[96]{0:T(512)(128)(4,1)S(1)} %iota_compare_fusion.1, s32[96]{0:T(128)S(1)} %get-tuple-element.18), kind=kOutput, calls=%fused_computation.95 | convolution fusion | flops 75497856 | bytes 12845536 | tf_op jit(solution)/shard_map/ik,kaf->iaf/dot_general | solution.py:25
  252.0 1.9 collective-permute-start
  253.9 2.5 collective-permute-done
  256.4 0.9 add_convert_fusion
  257.3 0.0 all-gather.9.cloned.1.call-update
  257.3 0.3 all-reduce.3.cloned.1.call-start
  257.6 0.7 iota_compare_fusion
  258.3 0.2 fusion.24
  258.5 0.2 fusion.27
  258.8 0.9 fusion.9
  259.7 78.0 %all-gather.9.cloned.1.call-done = bf16[8192,256]{1,0:T(8,128)(2,1)} async-done(((bf16[256,256]{1,0:T(8,128)(2,1)}), bf16[8192,256]{1,0:T(8,128)(2,1)}) %all-gather.9.cloned.1.call-update) | async-done | bytes 4194320 | tf_op jit(solution)/shard_map/all_gather | solution.py:62
  337.7 8.1 %gather_fusion.2 = bf16[96,128,256]{2,1,0:T(8,128)(2,1)} fusion(bf16[64,128,256]{2,1,0:T(8,128)(2,1)} %bitcast.143, s32[1024]{0:T(1024)S(1)} %pad_clamp_fusion), kind=kCustom, calls=%fused_computation.2 | custom fusion | bytes 12583296 | tf_op jit(solution)/shard_map/gather | solution.py:19
  345.8 10.1 %convolution_bitcast_fusion.1 = f32[96,128,256]{1,2,0:T(8,128)} fusion(bf16[96,128,256]{2,1,0:T(8,128)(2,1)} %gather_fusion.2, bf16[1,2,96,128,128]{4,3,2,1,0:T(8,128)(2,1)} %param.14), kind=kOutput, calls=%fused_computation.5 | convolution fusion | flops 805306368 | bytes 22020096 | tf_op jit(solution)/shard_map/kab,kbf->kaf/dot_general | solution.py:20
  355.9 12.8 %copy.44 = f32[96,128,256]{2,0,1:T(8,128)} copy(f32[96,128,256]{1,2,0:T(8,128)} %convolution_bitcast_fusion.1) | data formatting | bytes 25165824 | tf_op jit(solution)/shard_map/kab,kbf->kaf/dot_general | solution.py:20
  368.6 7.0 %fusion.61 = f32[2,128,256]{2,0,1:T(2,128)S(1)} fusion(f32[96,128,256]{2,0,1:T(8,128)} %copy.44, pred[96]{0:T(512)(128)(4,1)S(1)} %iota_compare_fusion, s32[96]{0:T(128)S(1)} %get-tuple-element.17), kind=kOutput, calls=%fused_computation.93 | convolution fusion | flops 75497856 | bytes 12845536 | tf_op jit(solution)/shard_map/ik,kaf->iaf/dot_general | solution.py:25
  375.7 0.9 fusion.11
  376.7 0.3 all-gather.11.cloned.1.call-start
  377.0 0.9 fusion.17
  378.0 0.9 multiply_bitcast_fusion
  378.9 0.8 maximum_bitcast_fusion
  379.8 141.9 %all-reduce.3.cloned.1.call-done = (f32[256,256]{0,1:T(8,128)}, f32[256,256]{0,1:T(8,128)}) async-done(((f32[256,256]{0,1:T(8,128)}, f32[256,256]{0,1:T(8,128)}), (f32[256,256]{0,1:T(8,128)}, f32[256,256]{0,1:T(8,128)})) %all-reduce.3.cloned.1.call-update) | async-done | bytes 524304 | tf_op jit(solution)/shard_map/psum | solution.py:56
  521.7 1.1 maximum_bitcast_fusion.1
  522.7 1.0 copy.50
  523.7 79.4 %all-gather.11.cloned.1.call-done = bf16[8192,256]{1,0:T(8,128)(2,1)} async-done(((bf16[256,256]{1,0:T(8,128)(2,1)}), bf16[8192,256]{1,0:T(8,128)(2,1)}) %all-gather.11.cloned.1.call-update) | async-done | bytes 4194320 | tf_op jit(solution)/shard_map/all_gather | solution.py:62
  603.1 8.1 %gather_fusion.3 = bf16[96,128,256]{2,1,0:T(8,128)(2,1)} fusion(bf16[64,128,256]{2,1,0:T(8,128)(2,1)} %bitcast.142, s32[1024]{0:T(1024)S(1)} %pad_clamp_fusion), kind=kCustom, calls=%fused_computation.3 | custom fusion | bytes 12583296 | tf_op jit(solution)/shard_map/gather | solution.py:19
  611.2 10.1 %convolution_bitcast_fusion = f32[96,128,256]{1,2,0:T(8,128)} fusion(bf16[96,128,256]{2,1,0:T(8,128)(2,1)} %gather_fusion.3, bf16[1,2,96,128,128]{4,3,2,1,0:T(8,128)(2,1)} %param.14), kind=kOutput, calls=%fused_computation.4 | convolution fusion | flops 805306368 | bytes 22020096 | tf_op jit(solution)/shard_map/kab,kbf->kaf/dot_general | solution.py:20
  621.3 12.8 %copy.47 = f32[96,128,256]{2,0,1:T(8,128)} copy(f32[96,128,256]{1,2,0:T(8,128)} %convolution_bitcast_fusion) | data formatting | bytes 25165824 | tf_op jit(solution)/shard_map/kab,kbf->kaf/dot_general | solution.py:20
  634.1 7.0 %fusion.59 = f32[2,128,256]{2,0,1:T(2,128)S(1)} fusion(f32[96,128,256]{2,0,1:T(8,128)} %copy.47, pred[96]{0:T(512)(128)(4,1)S(1)} %iota_compare_fusion, s32[96]{0:T(128)S(1)} %get-tuple-element.17), kind=kOutput, calls=%fused_computation.91 | convolution fusion | flops 75497856 | bytes 12845536 | tf_op jit(solution)/shard_map/ik,kaf->iaf/dot_general | solution.py:25
  641.1 0.7 maximum_bitcast_fusion.2
  (27 shorter events, 0.3 us)
Async XLA Ops:
  7.2 88.6 %all-gather.5.cloned.1.call-start = ((), (), s32[]{:S(2)}) async-start(), calls=%async_computation | async-start | bytes 4325376 | tf_op jit(solution)/shard_map/all_gather | solution.py:62
  9.4 204.6 %all-gather.7.cloned.1.call-start = ((), (), s32[]{:S(2)}) async-start(), calls=%async_computation.1 | async-start | bytes 4325376 | tf_op jit(solution)/shard_map/all_gather | solution.py:62
  126.7 7.1 %copy-start = (bf16[1,2,2,256,256]{4,3,2,1,0:T(8,128)(2,1)S(1)}, bf16[1,2,2,256,256]{4,3,2,1,0:T(8,128)(2,1)}, u32[]{:S(2)}) copy-start(bf16[1,2,2,256,256]{4,3,2,1,0:T(8,128)(2,1)} %param.12) | copy-start | bytes 1572868
  126.7 7.1 %copy-start.7 = (bf16[1,2,256,256]{3,2,1,0:T(8,128)(2,1)S(1)}, bf16[1,2,256,256]{3,2,1,0:T(8,128)(2,1)}, u32[]{:S(2)}) copy-start(bf16[1,2,256,256]{3,2,1,0:T(8,128)(2,1)} %param.13) | copy-start | bytes 786436
  134.8 202.9 %all-gather.9.cloned.1.call-start = ((), (), s32[]{:S(2)}) async-start(), calls=%async_computation.2 | async-start | bytes 4325376 | tf_op jit(solution)/shard_map/all_gather | solution.py:62
  244.9 11.6 %copy-start.5 = (bf16[256,256]{1,0:T(8,128)(2,1)S(1)}, bf16[256,256]{1,0:T(8,128)(2,1)}, u32[]{:S(2)}) copy-start(bf16[256,256]{1,0:T(8,128)(2,1)} %param.10) | copy-start | bytes 393220
  244.9 13.4 %copy-start.1 = (bf16[1,2,2,256,256]{4,3,2,1,0:T(8,128)(2,1)S(1)}, bf16[1,2,2,256,256]{4,3,2,1,0:T(8,128)(2,1)}, u32[]{:S(2)}) copy-start(bf16[1,2,2,256,256]{4,3,2,1,0:T(8,128)(2,1)} %param.11) | copy-start | bytes 1572868
  244.9 13.4 %copy-start.6 = (bf16[1,256,256]{2,1,0:T(8,128)(2,1)S(1)}, bf16[1,256,256]{2,1,0:T(8,128)(2,1)}, u32[]{:S(2)}) copy-start(bf16[1,256,256]{2,1,0:T(8,128)(2,1)} %param.9) | copy-start | bytes 393220
  252.0 4.4 collective-permute-start
  257.3 264.3 %all-reduce.3.cloned.1.call-start = ((), (), s32[]{:S(2)}) async-start(), calls=%async_computation.4 | async-start | bytes 1048576 | tf_op jit(solution)/shard_map/psum | solution.py:56
  368.6 9.3 %copy-start.2 = (bf16[256,256]{1,0:T(8,128)(2,1)S(1)}, bf16[256,256]{1,0:T(8,128)(2,1)}, u32[]{:S(2)}) copy-start(bf16[256,256]{1,0:T(8,128)(2,1)} %fusion.15) | copy-start | bytes 393220
  368.6 9.3 %copy-start.3 = (bf16[256,256]{1,0:T(8,128)(2,1)S(1)}, bf16[256,256]{1,0:T(8,128)(2,1)}, u32[]{:S(2)}) copy-start(bf16[256,256]{1,0:T(8,128)(2,1)} %fusion.16) | copy-start | bytes 393220
  368.6 9.3 %copy-start.4 = (bf16[256,256]{1,0:T(8,128)(2,1)S(1)}, bf16[256,256]{1,0:T(8,128)(2,1)}, u32[]{:S(2)}) copy-start(bf16[256,256]{1,0:T(8,128)(2,1)} %add_convert_fusion) | copy-start | bytes 393220
  376.7 226.5 %all-gather.11.cloned.1.call-start = ((), (), s32[]{:S(2)}) async-start(), calls=%async_computation.3 | async-start | bytes 4325376 | tf_op jit(solution)/shard_map/all_gather | solution.py:62
Sparse Core Ops, SparseCore 0:
  11.2 84.5 all-gather.4
  134.9 78.9 all-gather.6
  257.5 80.1 all-gather.8
  376.8 144.8 all-reduce.2
  524.5 78.6 all-gather.10
where the time goes:
time: 649 us; the launch traced here: 648 us
  waiting for transfers between devices  464 us (71%)
  local copies, waits for them, and re-layouts  86.5 us (13%)
  matrix products  75.5 us (12%)
  between operations  14.2 us (2%)
    all_gather x4, waiting for transfers between devices, shards(): gathered = lax.all_gather(image, 'rows', axis=0, tiled=True)  319 us
    psum x1, waiting for transfers between devices, shards(): weight_acc[layer] = weight_acc[layer] + lax.psum(term, 'rows')  142 us
    dot_general x4, local copies, waits for them, and re-layouts, tile_product(): jnp.einsum('kab,kbf->kaf', values, blocks, preferred_element_type=jnp.flo...  51 us
    dot_general x4, matrix products, tile_product(): jnp.einsum('kab,kbf->kaf', values, blocks, preferred_element_type=jnp.flo...  40.3 us
    gather x4, local copies, waits for them, and re-layouts, tile_product(): blocks = gathered.reshape(-1, tile, width)[index]  32.4 us
    dot_general x4, matrix products, tile_product(): jnp.einsum('ik,kaf->iaf', select, products, precision=lax.Precision.HIGHEST)  28.2 us
  transfers between devices with their start and end apart: 6, of which 6 were waited for; matrix products, arithmetic and copies ran while one was open for 2% of the time, Pallas kernels for 0%

commit v1 on v0

--- a/solution.py
+++ b/solution.py
@@ -59,7 +59,9 @@
                 + beta * jnp.dot(masked, weight.T, preferred_element_type=jnp.float32)
             ).astype(jnp.bfloat16)
             toward = toward + ALPHA * image.astype(jnp.float32)
-            gathered = lax.all_gather(image, "rows", axis=0, tiled=True)
+            gathered = jnp.concatenate(
+                lax.all_to_all(jnp.stack([image] * lax.axis_size("rows")), "rows", 0, 0), axis=0
+            )
             spread = tile_product(
                 gathered, tile_vals[0, tick], tile_row[0, tick], columns, count, row_tiles
             )

time: 649 us -> 681 us (1.049)
  blocking collectives: 0 us -> 101 us
  waiting for transfers between devices: 464 us -> 367 us
  starting transfers between devices: 2.79 us -> 28.6 us
    all_gather x4 -> x0, waiting for transfers between devices: 319 us -> none  [shards(): gathered = lax.all_gather(image, 'rows', axis=0, tiled=True)]
    all_to_all x0 -> x3, waiting for transfers between devices: none -> 190 us  [shards(): lax.all_to_all(jnp.stack([image] * lax.axis_size('rows')), 'rows', 0, 0)]
    all_to_all x0 -> x1, blocking collectives: none -> 101 us  [shards(): lax.all_to_all(jnp.stack([image] * lax.axis_size('rows')), 'rows', 0, 0)]
    psum x1, waiting for transfers between devices: 142 us -> 174 us  [shards(): weight_acc[layer] = weight_acc[layer] + lax.psum(term, 'rows')]
    all_to_all x0 -> x3, starting transfers between devices: none -> 26.3 us  [shards(): lax.all_to_all(jnp.stack([image] * lax.axis_size('rows')), 'rows', 0, 0)]
    another operation x0 -> x4, local copies, waits for them, and re-layouts: none -> 7.82 us  [shards(): jnp.stack([image] * lax.axis_size('rows'))]
  transfers between devices with their start and end apart: 6 -> 5, of which waited for: 6 -> 4; matrix products, arithmetic and copies ran while one was open for 2% -> 1% of each run, Pallas kernels for 0% -> 0%
where the time goes in v1:
time: 681 us; the launch traced here: 680 us
  waiting for transfers between devices  367 us (54%)
  blocking collectives  101 us (15%)
  local copies, waits for them, and re-layouts  92.9 us (14%)
  matrix products  72.8 us (11%)
  starting transfers between devices  28.6 us (4%)
  between operations  14.5 us (2%)
    all_to_all x3, waiting for transfers between devices, shards(): lax.all_to_all(jnp.stack([image] * lax.axis_size('rows')), 'rows', 0, 0)  190 us
    psum x1, waiting for transfers between devices, shards(): weight_acc[layer] = weight_acc[layer] + lax.psum(term, 'rows')  174 us
    all_to_all x1, blocking collectives, shards(): lax.all_to_all(jnp.stack([image] * lax.axis_size('rows')), 'rows', 0, 0)  101 us
    dot_general x4, local copies, waits for them, and re-layouts, tile_product(): jnp.einsum('kab,kbf->kaf', values, blocks, preferred_element_type=jnp.flo...  51 us
    dot_general x4, matrix products, tile_product(): jnp.einsum('kab,kbf->kaf', values, blocks, preferred_element_type=jnp.flo...  40.4 us
    gather x4, local copies, waits for them, and re-layouts, tile_product(): blocks = gathered.reshape(-1, tile, width)[index]  32.5 us
    dot_general x4, matrix products, tile_product(): jnp.einsum('ik,kaf->iaf', select, products, precision=lax.Precision.HIGHEST)  28.1 us
    all_to_all x3, starting transfers between devices, shards(): lax.all_to_all(jnp.stack([image] * lax.axis_size('rows')), 'rows', 0, 0)  26.3 us
  transfers between devices with their start and end apart: 5, of which 4 were waited for; matrix products, arithmetic and copies ran while one was open for 1% of the time, Pallas kernels for 0%

profile of v1, /device:TPU:8, one launch (start us, length us, event | category | flops | bytes accessed | tf_op | source)
XLA Modules:
  0.0 680.3 jit_solution(43178214722752357)
XLA Ops:
  7.3 1.4 fusion.15
  8.7 0.0 copy-start.4
  8.7 0.0 copy-start.5
  8.7 2.5 stack.22
  11.1 11.4 %all-to-all-start = ((bf16[32,256,256]{2,1,0:T(8,128)(2,1)}), bf16[32,256,256]{2,1,0:T(8,128)(2,1)}, u32[]{:S(2)}, u32[]{:S(2)}) async-start(bf16[32,256,256]{2,1,0:T(8,128)(2,1)} %stack.22), calls=%async_computation | async-start | bytes 8388608 | tf_op jit(solution)/shard_map/all_to_all | solution.py:63
  22.7 0.6 fusion.83
  23.3 0.6 iota_compare_fusion.1
  24.0 95.8 %all-to-all-done = bf16[32,256,256]{2,1,0:T(8,128)(2,1)} async-done(((bf16[32,256,256]{2,1,0:T(8,128)(2,1)}), bf16[32,256,256]{2,1,0:T(8,128)(2,1)}, u32[]{:S(2)}, u32[]{:S(2)}) %all-to-all-start) | async-done | bytes 4194336 | tf_op jit(solution)/shard_map/all_to_all | solution.py:63
  119.8 8.1 %gather_fusion = bf16[96,128,256]{2,1,0:T(8,128)(2,1)} fusion(bf16[64,128,256]{2,1,0:T(8,128)(2,1)} %bitcast.9, s32[1024]{0:T(1024)S(1)} %pad_clamp_fusion.1), kind=kCustom, calls=%fused_computation | custom fusion | bytes 12583296 | tf_op jit(solution)/shard_map/gather | solution.py:19
  127.9 10.1 %convolution_bitcast_fusion.3 = f32[96,128,256]{1,2,0:T(8,128)} fusion(bf16[96,128,256]{2,1,0:T(8,128)(2,1)} %gather_fusion, bf16[1,2,96,128,128]{4,3,2,1,0:T(8,128)(2,1)} %param.14), kind=kOutput, calls=%fused_computation.7 | convolution fusion | flops 805306368 | bytes 22020096 | tf_op jit(solution)/shard_map/kab,kbf->kaf/dot_general | solution.py:20
  138.0 12.7 %copy.38 = f32[96,128,256]{2,0,1:T(8,128)} copy(f32[96,128,256]{1,2,0:T(8,128)} %convolution_bitcast_fusion.3) | data formatting | bytes 25165824 | tf_op jit(solution)/shard_map/kab,kbf->kaf/dot_general | solution.py:20
  150.8 7.1 %fusion.65 = f32[2,128,256]{2,0,1:T(2,128)S(1)} fusion(f32[96,128,256]{2,0,1:T(8,128)} %copy.38, pred[96]{0:T(512)(128)(4,1)S(1)} %iota_compare_fusion.1, s32[96]{0:T(128)S(1)} %get-tuple-element.18), kind=kOutput, calls=%fused_computation.97 | convolution fusion | flops 75497856 | bytes 12845536 | tf_op jit(solution)/shard_map/ik,kaf->iaf/dot_general | solution.py:25
  157.9 0.2 fusion.16
  158.1 0.5 stack.23
  158.6 100.8 %all_to_all.20 = bf16[32,256,256]{2,1,0:T(8,128)(2,1)} all-to-all(bf16[32,256,256]{2,1,0:T(8,128)(2,1)S(1)} %stack.23), channel_id=1, replica_groups=mesh['section'=8,'rows'=32] {'rows'}, dimensions={0} | all-to-all | bytes 8388608 | tf_op jit(solution)/shard_map/all_to_all | solution.py:63
  259.4 8.1 %gather_fusion.1 = bf16[96,128,256]{2,1,0:T(8,128)(2,1)} fusion(bf16[64,128,256]{2,1,0:T(8,128)(2,1)} %bitcast.141, s32[1024]{0:T(1024)S(1)} %pad_clamp_fusion.1), kind=kCustom, calls=%fused_computation.1 | custom fusion | bytes 12583296 | tf_op jit(solution)/shard_map/gather | solution.py:19
  267.5 10.1 %convolution_bitcast_fusion.2 = f32[96,128,256]{1,2,0:T(8,128)} fusion(bf16[96,128,256]{2,1,0:T(8,128)(2,1)} %gather_fusion.1, bf16[1,2,96,128,128]{4,3,2,1,0:T(8,128)(2,1)} %param.14), kind=kOutput, calls=%fused_computation.6 | convolution fusion | flops 805306368 | bytes 22020096 | tf_op jit(solution)/shard_map/kab,kbf->kaf/dot_general | solution.py:20
  277.6 12.7 %copy.41 = f32[96,128,256]{2,0,1:T(8,128)} copy(f32[96,128,256]{1,2,0:T(8,128)} %convolution_bitcast_fusion.2) | data formatting | bytes 25165824 | tf_op jit(solution)/shard_map/kab,kbf->kaf/dot_general | solution.py:20
  290.4 7.0 %fusion.63 = f32[2,128,256]{2,0,1:T(2,128)S(1)} fusion(f32[96,128,256]{2,0,1:T(8,128)} %copy.41, pred[96]{0:T(512)(128)(4,1)S(1)} %iota_compare_fusion.1, s32[96]{0:T(128)S(1)} %get-tuple-element.18), kind=kOutput, calls=%fused_computation.95 | convolution fusion | flops 75497856 | bytes 12845536 | tf_op jit(solution)/shard_map/ik,kaf->iaf/dot_general | solution.py:25
  297.5 1.9 collective-permute-start
  299.4 2.5 collective-permute-done
  301.9 0.2 add_convert_fusion
  302.2 2.5 stack.24
  304.6 5.3 all-to-all-start.2
  309.9 0.7 iota_compare_fusion
  310.6 94.6 %all-to-all-done.2 = bf16[32,256,256]{2,1,0:T(8,128)(2,1)} async-done(((bf16[32,256,256]{2,1,0:T(8,128)(2,1)}), bf16[32,256,256]{2,1,0:T(8,128)(2,1)}, u32[]{:S(2)}, u32[]{:S(2)}) %all-to-all-start.2) | async-done | bytes 4194336 | tf_op jit(solution)/shard_map/all_to_all | solution.py:63
  405.2 8.1 %gather_fusion.2 = bf16[96,128,256]{2,1,0:T(8,128)(2,1)} fusion(bf16[64,128,256]{2,1,0:T(8,128)(2,1)} %bitcast.27, s32[1024]{0:T(1024)S(1)} %pad_clamp_fusion), kind=kCustom, calls=%fused_computation.2 | custom fusion | bytes 12583296 | tf_op jit(solution)/shard_map/gather | solution.py:19
  413.3 10.1 %convolution_bitcast_fusion.1 = f32[96,128,256]{1,2,0:T(8,128)} fusion(bf16[96,128,256]{2,1,0:T(8,128)(2,1)} %gather_fusion.2, bf16[1,2,96,128,128]{4,3,2,1,0:T(8,128)(2,1)} %param.14), kind=kOutput, calls=%fused_computation.5 | convolution fusion | flops 805306368 | bytes 22020096 | tf_op jit(solution)/shard_map/kab,kbf->kaf/dot_general | solution.py:20
  423.4 12.7 %copy.44 = f32[96,128,256]{2,0,1:T(8,128)} copy(f32[96,128,256]{1,2,0:T(8,128)} %convolution_bitcast_fusion.1) | data formatting | bytes 25165824 | tf_op jit(solution)/shard_map/kab,kbf->kaf/dot_general | solution.py:20
  436.2 7.0 %fusion.61 = f32[2,128,256]{2,0,1:T(2,128)S(1)} fusion(f32[96,128,256]{2,0,1:T(8,128)} %copy.44, pred[96]{0:T(512)(128)(4,1)S(1)} %iota_compare_fusion, s32[96]{0:T(128)S(1)} %get-tuple-element.17), kind=kOutput, calls=%fused_computation.93 | convolution fusion | flops 75497856 | bytes 12845536 | tf_op jit(solution)/shard_map/ik,kaf->iaf/dot_general | solution.py:25
  443.2 0.2 fusion.17
  443.5 2.5 stack.25
  445.9 9.6 %all-to-all-start.3 = ((bf16[32,256,256]{2,1,0:T(8,128)(2,1)}), bf16[32,256,256]{2,1,0:T(8,128)(2,1)}, u32[]{:S(2)}, u32[]{:S(2)}) async-start(bf16[32,256,256]{2,1,0:T(8,128)(2,1)} %stack.25), calls=%async_computation.3 | async-start | bytes 8388608 | tf_op jit(solution)/shard_map/all_to_all | solution.py:63
  455.5 0.3 all-reduce.3.cloned.1.call-start
  455.8 0.2 fusion.24
  456.1 0.2 fusion.27
  456.3 0.9 fusion.9
  457.2 0.9 fusion.11
  458.2 0.0 all-reduce.3.cloned.1.call-update
  458.3 0.8 maximum_bitcast_fusion
  459.1 173.6 %all-reduce.3.cloned.1.call-done = (f32[256,256]{0,1:T(8,128)}, f32[256,256]{0,1:T(8,128)}) async-done(((f32[256,256]{0,1:T(8,128)}, f32[256,256]{0,1:T(8,128)}), (f32[256,256]{0,1:T(8,128)}, f32[256,256]{0,1:T(8,128)})) %all-reduce.3.cloned.1.call-update) | async-done | bytes 524304 | tf_op jit(solution)/shard_map/psum | solution.py:56
  632.7 1.1 maximum_bitcast_fusion.1
  633.8 1.0 copy.50
  634.8 8.1 %gather_fusion.3 = bf16[96,128,256]{2,1,0:T(8,128)(2,1)} fusion(bf16[64,128,256]{2,1,0:T(8,128)(2,1)} %bitcast.35, s32[1024]{0:T(1024)S(1)} %pad_clamp_fusion), kind=kCustom, calls=%fused_computation.3 | custom fusion | bytes 12583296 | tf_op jit(solution)/shard_map/gather | solution.py:19
  642.9 10.1 %convolution_bitcast_fusion = f32[96,128,256]{1,2,0:T(8,128)} fusion(bf16[96,128,256]{2,1,0:T(8,128)(2,1)} %gather_fusion.3, bf16[1,2,96,128,128]{4,3,2,1,0:T(8,128)(2,1)} %param.14), kind=kOutput, calls=%fused_computation.4 | convolution fusion | flops 805306368 | bytes 22020096 | tf_op jit(solution)/shard_map/kab,kbf->kaf/dot_general | solution.py:20
  653.0 12.7 %copy.47 = f32[96,128,256]{2,0,1:T(8,128)} copy(f32[96,128,256]{1,2,0:T(8,128)} %convolution_bitcast_fusion) | data formatting | bytes 25165824 | tf_op jit(solution)/shard_map/kab,kbf->kaf/dot_general | solution.py:20
  665.7 7.0 %fusion.59 = f32[2,128,256]{2,0,1:T(2,128)S(1)} fusion(f32[96,128,256]{2,0,1:T(8,128)} %copy.47, pred[96]{0:T(512)(128)(4,1)S(1)} %iota_compare_fusion, s32[96]{0:T(128)S(1)} %get-tuple-element.17), kind=kOutput, calls=%fused_computation.91 | convolution fusion | flops 75497856 | bytes 12845536 | tf_op jit(solution)/shard_map/ik,kaf->iaf/dot_general | solution.py:25
  672.7 0.7 maximum_bitcast_fusion.2
  (26 shorter events, 0.3 us)
Async XLA Ops:
  8.7 14.0 %copy-start.4 = (s32[1,2,1]{1,2,0:T(1,128)S(1)}, s32[1,2,1]{1,2,0:T(1,128)}, u32[]{:S(2)}) copy-start(s32[1,2,1]{1,2,0:T(1,128)} %param.17) | copy-start | bytes 28
  8.7 15.3 %copy-start.5 = (s32[1,2,96]{2,1,0:T(2,128)S(1)}, s32[1,2,96]{2,1,0:T(2,128)}, u32[]{:S(2)}) copy-start(s32[1,2,96]{2,1,0:T(2,128)} %param.16) | copy-start | bytes 2308
  8.7 15.3 %copy-start.6 = (s32[1,2,96]{2,1,0:T(2,128)S(1)}, s32[1,2,96]{2,1,0:T(2,128)}, u32[]{:S(2)}) copy-start(s32[1,2,96]{2,1,0:T(2,128)} %param.15) | copy-start | bytes 2308
  11.1 108.7 %all-to-all-start = ((bf16[32,256,256]{2,1,0:T(8,128)(2,1)}), bf16[32,256,256]{2,1,0:T(8,128)(2,1)}, u32[]{:S(2)}, u32[]{:S(2)}) async-start(bf16[32,256,256]{2,1,0:T(8,128)(2,1)} %stack.22), calls=%async_computation | async-start | bytes 8388608 | tf_op jit(solution)/shard_map/all_to_all | solution.py:63
  150.8 7.1 %copy-start = (bf16[1,2,2,256,256]{4,3,2,1,0:T(8,128)(2,1)S(1)}, bf16[1,2,2,256,256]{4,3,2,1,0:T(8,128)(2,1)}, u32[]{:S(2)}) copy-start(bf16[1,2,2,256,256]{4,3,2,1,0:T(8,128)(2,1)} %param.12) | copy-start | bytes 1572868
  150.8 7.1 %copy-start.7 = (bf16[1,2,256,256]{3,2,1,0:T(8,128)(2,1)S(1)}, bf16[1,2,256,256]{3,2,1,0:T(8,128)(2,1)}, u32[]{:S(2)}) copy-start(bf16[1,2,256,256]{3,2,1,0:T(8,128)(2,1)} %param.13) | copy-start | bytes 786436
  290.4 11.5 %copy-start.2 = (bf16[256,256]{1,0:T(8,128)(2,1)S(1)}, bf16[256,256]{1,0:T(8,128)(2,1)}, u32[]{:S(2)}) copy-start(bf16[256,256]{1,0:T(8,128)(2,1)} %param.10) | copy-start | bytes 393220
  297.5 4.4 collective-permute-start
  304.6 100.6 %all-to-all-start.2 = ((bf16[32,256,256]{2,1,0:T(8,128)(2,1)}), bf16[32,256,256]{2,1,0:T(8,128)(2,1)}, u32[]{:S(2)}, u32[]{:S(2)}) async-start(bf16[32,256,256]{2,1,0:T(8,128)(2,1)} %stack.24), calls=%async_computation.2 | async-start | bytes 8388608 | tf_op jit(solution)/shard_map/all_to_all | solution.py:63
  443.4 12.4 %copy-start.1 = (bf16[1,2,2,256,256]{4,3,2,1,0:T(8,128)(2,1)S(1)}, bf16[1,2,2,256,256]{4,3,2,1,0:T(8,128)(2,1)}, u32[]{:S(2)}) copy-start(bf16[1,2,2,256,256]{4,3,2,1,0:T(8,128)(2,1)} %param.11) | copy-start | bytes 1572868
  443.5 12.4 %copy-start.3 = (bf16[1,256,256]{2,1,0:T(8,128)(2,1)S(1)}, bf16[1,256,256]{2,1,0:T(8,128)(2,1)}, u32[]{:S(2)}) copy-start(bf16[1,256,256]{2,1,0:T(8,128)(2,1)} %param.9) | copy-start | bytes 393220
  445.9 188.8 %all-to-all-start.3 = ((bf16[32,256,256]{2,1,0:T(8,128)(2,1)}), bf16[32,256,256]{2,1,0:T(8,128)(2,1)}, u32[]{:S(2)}, u32[]{:S(2)}) async-start(bf16[32,256,256]{2,1,0:T(8,128)(2,1)} %stack.25), calls=%async_computation.3 | async-start | bytes 8388608 | tf_op jit(solution)/shard_map/all_to_all | solution.py:63
  455.5 177.2 %all-reduce.3.cloned.1.call-start = ((), (), s32[]{:S(2)}) async-start(), calls=%async_computation.4 | async-start | bytes 1048576 | tf_op jit(solution)/shard_map/psum | solution.py:56
Sparse Core Ops, SparseCore 0:
  460.4 172.2 all-reduce.2
